TPU v7x, 512 devices: a whole 4x8x8 slice. The times are simulated.
512 devices in a mesh: ctx: 16 (over y, core), head: 32 (over z, x).
Axes of the slice: x: 4, y: 8, z: 8, core: 2. Of those that a mesh axis runs over, the one named last changes fastest.
Arguments:
- query_rows: bfloat16 [6144, 64, 128], P('ctx', 'head'), may hold values from -1.75 to 1.75
- key_matrix: bfloat16 [6144, 64, 128], P('ctx', 'head'), may hold values from -1.75 to 1.75
- value_rows: bfloat16 [6144, 64, 128], P('ctx', 'head'), may hold values from -55 to 55
- decay_log: float32 [6144, 64], P('ctx', 'head'), may hold values from -0.6 to 0
- norm_gain: float32 [64, 128], P('head'), may hold values from 0.1 to 1.9
- grad_out: bfloat16 [6144, 64, 128], P('ctx', 'head'), may hold values from -6 to 6
Outputs:
- output: bfloat16 [6144, 64, 128], P('ctx', 'head')
- grad_query: bfloat16 [6144, 64, 128], P('ctx', 'head')
- grad_key: bfloat16 [6144, 64, 128], P('ctx', 'head')
- grad_value: bfloat16 [6144, 64, 128], P('ctx', 'head')
All inputs are finite; a program needn't handle non-finite values.
Results may differ from a plain program's by a relative error of at most 0.019.
Values sent between devices are 32-bit elements; how exact they have to be, the bound alone decides.
A program may use at most 64 MiB of HBM per device.

v0:
```python
import jax
import jax.numpy as jnp
from jax import lax
from jax.sharding import PartitionSpec as P

GROUP = 128
epsilon = 1e-06


def weigh_gathered(gathered, log_rates, position, forward):
    device_ranks = jnp.arange(log_rates.shape[0], dtype=jnp.int32)
    running = jnp.cumsum(log_rates, axis=0)
    own_total = running[position]
    if forward:
        keep_mask = device_ranks < position
        spread = (own_total - log_rates[position])[None, :] - running
    else:
        keep_mask = device_ranks > position
        spread = running - log_rates - own_total[None, :]
    keep_mask = keep_mask[:, None]
    factors = jnp.where(keep_mask, jnp.exp(jnp.where(keep_mask, spread, 0.0)), 0.0)
    return jnp.einsum("nh,nhde->hde", factors, gathered, precision=lax.Precision.HIGHEST)


def per_device(query_rows, key_matrix, value_rows, decay_log, norm_gain, grad_out):
    token_count, head_count, head_size = query_rows.shape
    num_blocks = token_count // GROUP
    query_blocks = query_rows.reshape(num_blocks, GROUP, head_count, head_size)
    key_blocks = key_matrix.reshape(num_blocks, GROUP, head_count, head_size)
    value_blocks = value_rows.reshape(num_blocks, GROUP, head_count, head_size)
    cumulative = jnp.cumsum(decay_log.reshape(num_blocks, GROUP, head_count), axis=1)
    block_total = cumulative[:, -1, :]
    cum_major = jnp.transpose(cumulative, (0, 2, 1))
    row_ids = lax.broadcasted_iota(jnp.int32, (GROUP, GROUP), 0)
    col_ids = lax.broadcasted_iota(jnp.int32, (GROUP, GROUP), 1)
    causal = (row_ids >= col_ids)[None, None]
    spread = cum_major[:, :, :, None] - cum_major[:, :, None, :]
    mask_weight = jnp.where(causal, jnp.exp(jnp.where(causal, spread, 0.0)), 0.0)
    scores = jnp.einsum(
        "cihd,cjhd->chij", query_blocks, key_blocks, preferred_element_type=jnp.float32
    )
    attn_weights = (scores * mask_weight).astype(jnp.bfloat16)
    local_part = jnp.einsum(
        "chij,cjhd->cihd", attn_weights, value_blocks, preferred_element_type=jnp.float32
    )

    def advance(carry_state, pieces):
        key_part, value_part, cum_part, total_part = pieces
        decayed = (key_part * jnp.exp(total_part[None, :] - cum_part)[:, :, None]).astype(
            jnp.bfloat16
        )
        fresh_term = jnp.einsum(
            "ihd,ihe->hde", decayed, value_part, preferred_element_type=jnp.float32
        )
        return (jnp.exp(total_part)[:, None, None] * carry_state + fresh_term, carry_state)

    zero_state = jnp.zeros((head_count, head_size, head_size), jnp.float32)
    end_state, local_states = lax.scan(
        advance, zero_state, (key_blocks, value_blocks, cumulative, block_total)
    )
    total_log = jnp.sum(block_total, axis=0)
    position = lax.axis_index("ctx")
    gathered, log_rates = (
        lax.all_gather(end_state[None], "ctx", axis=0, tiled=True),
        lax.all_gather(total_log[None], "ctx", axis=0, tiled=True),
    )
    incoming = weigh_gathered(gathered, log_rates, position, True)
    before = jnp.cumsum(block_total, axis=0) - block_total
    state_bf = (local_states + jnp.exp(before)[:, :, None, None] * incoming[None]).astype(
        jnp.bfloat16
    )
    carried_part = (
        jnp.einsum("cihd,chde->cihe", query_blocks, state_bf, preferred_element_type=jnp.float32)
        * jnp.exp(cumulative)[:, :, :, None]
    )
    attention = (
        (local_part + carried_part).astype(jnp.bfloat16).reshape(token_count, head_count, head_size)
    )
    attn_f = attention.astype(jnp.float32)
    grad_f = grad_out.astype(jnp.float32)
    features = head_count * lax.axis_size("head") * head_size
    square_sum = lax.psum(jnp.sum(attn_f * attn_f, axis=(1, 2)), "head")
    inv_rms = lax.rsqrt(square_sum / features + epsilon)
    output = (attn_f * inv_rms[:, None, None] * norm_gain[None]).astype(jnp.bfloat16)
    scaled_grad = norm_gain[None] * (grad_f + output.astype(jnp.float32))
    inner = lax.psum(jnp.sum(scaled_grad * attn_f, axis=(1, 2)), "head")
    grad_attention = (
        inv_rms[:, None, None] * scaled_grad
        - attn_f * (inv_rms**3 * inner / features)[:, None, None]
    ).astype(jnp.bfloat16)
    grad_blocks = grad_attention.reshape(num_blocks, GROUP, head_count, head_size)
    grad_dots = jnp.einsum(
        "cihe,cjhe->chij", grad_blocks, value_blocks, preferred_element_type=jnp.float32
    )
    grad_scores = (grad_dots * mask_weight).astype(jnp.bfloat16)
    query_local = jnp.einsum(
        "chij,cjhd->cihd", grad_scores, key_blocks, preferred_element_type=jnp.float32
    )
    key_local = jnp.einsum(
        "chij,cihd->cjhd", grad_scores, query_blocks, preferred_element_type=jnp.float32
    )
    value_local = jnp.einsum(
        "chij,cihe->cjhe", attn_weights, grad_blocks, preferred_element_type=jnp.float32
    )
    query_carried = (
        jnp.einsum("cihe,chde->cihd", grad_blocks, state_bf, preferred_element_type=jnp.float32)
        * jnp.exp(cumulative)[:, :, :, None]
    )

    def retreat(carry_state, pieces):
        query_part, grad_part, cum_part, total_part = pieces
        decayed = (query_part * jnp.exp(cum_part)[:, :, None]).astype(jnp.bfloat16)
        fresh_term = jnp.einsum(
            "ihd,ihe->hde", decayed, grad_part, preferred_element_type=jnp.float32
        )
        return (jnp.exp(total_part)[:, None, None] * carry_state + fresh_term, carry_state)

    start_state, local_back = lax.scan(
        retreat, zero_state, (query_blocks, grad_blocks, cumulative, block_total), reverse=True
    )
    gathered_back, log_back = (
        lax.all_gather(start_state[None], "ctx", axis=0, tiled=True),
        lax.all_gather(total_log[None], "ctx", axis=0, tiled=True),
    )
    arriving = weigh_gathered(gathered_back, log_back, position, False)
    after = total_log[None, :] - jnp.cumsum(block_total, axis=0)
    back_bf = (local_back + jnp.exp(after)[:, :, None, None] * arriving[None]).astype(jnp.bfloat16)
    tail = jnp.exp(block_total[:, None, :] - cumulative)[:, :, :, None]
    key_carried = (
        jnp.einsum("cihe,chde->cihd", value_blocks, back_bf, preferred_element_type=jnp.float32)
        * tail
    )
    value_carried = (
        jnp.einsum("cihd,chde->cihe", key_blocks, back_bf, preferred_element_type=jnp.float32)
        * tail
    )
    shape_out = (token_count, head_count, head_size)
    grad_query = (query_local + query_carried).astype(jnp.bfloat16).reshape(shape_out)
    grad_key = (key_local + key_carried).astype(jnp.bfloat16).reshape(shape_out)
    grad_value = (value_local + value_carried).astype(jnp.bfloat16).reshape(shape_out)
    return (output, grad_query, grad_key, grad_value)


def solution(mesh):
    placed = (
        P("ctx", "head", None),
        P("ctx", "head", None),
        P("ctx", "head", None),
        P("ctx", "head"),
        P("head", None),
        P("ctx", "head", None),
    )
    return jax.shard_map(
        per_device,
        mesh=mesh,
        in_specs=placed,
        out_specs=(
            P("ctx", "head", None),
            P("ctx", "head", None),
            P("ctx", "head", None),
            P("ctx", "head", None),
        ),
        check_vma=False,
    )
```

profile of v0, /device:TPU:1, one launch (start us, length us, event | category | flops | bytes accessed | tf_op | source)
XLA Modules:
  0.0 262.6 jit_solution(10493295506692607835)
XLA Ops:
  7.2 0.8 copy.129
  8.6 1.0 copy.79
  9.5 1.0 copy.85
  10.6 1.4 while.30
  12.0 0.6 copy-done.1
  12.9 1.3 dynamic-slice
  15.1 29.7 %all-reduce = f32[32]{0:T(128)S(1)} all-reduce(f32[32]{0:T(128)S(1)} %dynamic-update-slice), channel_id=2, replica_groups=mesh['ctx'=16,'head'=32] {'ctx'}, use_global_device_ids=true, to_apply=%add | all-reduce | flops 32 | bytes 256
  45.9 14.7 %all-gather.6.cloned.1.call-done = f32[32,128,128]{2,1,0:T(8,128)} async-done(((f32[2,128,128]{2,1,0:T(8,128)}), f32[32,128,128]{2,1,0:T(8,128)}) %all-gather.6.cloned.1.call-update) | async-done | bytes 2097168 | tf_op jit(solution)/shard_map/all_gather | solution.py:64
  60.6 3.8 %fusion.24 = f32[2,1,128,128]{3,1,2,0:T(1,128)S(1)} fusion(f32[16,2,1,1]{0,2,3,1:T(1,128)S(1)} %copy.121, f32[16,2,128,128]{3,2,1,0:T(8,128)} %bitcast.159), kind=kOutput, calls=%fused_computation.34 | convolution fusion | flops 6291456 | bytes 2228352 | tf_op jit(solution)/shard_map/nh,nhde->hde/dot_general | solution.py:22
  64.4 0.3 fusion.27
  64.6 0.3 multiply_reduce_fusion
  65.0 61.6 %psum.14 = f32[384]{0:T(512)S(1)} all-reduce(f32[384]{0:T(512)S(1)} %bitcast.171), channel_id=1, replica_groups=mesh['ctx'=16,'head'=32] {'head'}, use_global_device_ids=true, to_apply=%region_7.8 | all-reduce | flops 384 | bytes 3072 | tf_op jit(solution)/shard_map/psum | solution.py:82
  126.9 56.2 %psum.15 = f32[384]{0:T(512)S(1)} all-reduce(f32[384]{0:T(512)S(1)} %fusion.43), channel_id=1, replica_groups=mesh['ctx'=16,'head'=32] {'head'}, use_global_device_ids=true, to_apply=%region_9.10 | all-reduce | flops 384 | bytes 3072 | tf_op jit(solution)/shard_map/psum | solution.py:86
  183.4 1.2 while.31
  184.6 0.6 copy-done
  185.6 0.9 copy.117
  186.7 0.3 fusion.31
  187.3 0.9 copy.118
  188.2 60.8 %all-gather.8.cloned.1.call-done = f32[32,128,128]{2,1,0:T(8,128)} async-done(((f32[2,128,128]{2,1,0:T(8,128)}), f32[32,128,128]{2,1,0:T(8,128)}) %all-gather.8.cloned.1.call-update) | async-done | bytes 2097168 | tf_op jit(solution)/shard_map/all_gather | solution.py:122
  249.0 3.8 %fusion.22 = f32[2,1,128,128]{3,1,2,0:T(1,128)S(1)} fusion(f32[16,2,1,1]{0,2,3,1:T(1,128)S(1)} %copy.125, f32[16,2,128,128]{3,2,1,0:T(8,128)} %bitcast.160), kind=kOutput, calls=%fused_computation.32 | convolution fusion | flops 6291456 | bytes 2228352 | tf_op jit(solution)/shard_map/nh,nhde->hde/dot_general | solution.py:22
  252.8 0.3 fusion.29
  253.1 0.3 fusion.26
  253.7 0.9 copy.119
  254.9 0.9 copy.120
  (91 shorter events, 6.3 us)
Async XLA Ops:
  7.2 53.4 %all-gather.6.cloned.1.call-start = ((), (), s32[]{:S(2)}) async-start(), calls=%async_computation | async-start | bytes 2228224 | tf_op jit(solution)/shard_map/all_gather | solution.py:64
  10.6 2.3 copy-start.3
  12.0 0.7 copy-start.1
  12.6 236.4 %all-gather.8.cloned.1.call-start = ((), (), s32[]{:S(2)}) async-start(), calls=%async_computation.1 | async-start | bytes 2228224 | tf_op jit(solution)/shard_map/all_gather | solution.py:122
  64.3 62.3 %copy-start.2 = (bf16[384,2,128]{2,1,0:T(2,128)(2,1)S(1)}, bf16[384,2,128]{2,1,0:T(2,128)(2,1)}, u32[]{:S(2)}) copy-start(bf16[384,2,128]{2,1,0:T(2,128)(2,1)} %param.15) | copy-start | bytes 589828
  64.4 62.3 %copy-start.4 = (f32[2,128]{1,0:T(2,128)S(1)}, f32[2,128]{1,0:T(2,128)}, u32[]{:S(2)}) copy-start(f32[2,128]{1,0:T(2,128)} %param.14) | copy-start | bytes 3076
  184.6 0.7 copy-start
Sparse Core Ops, SparseCore 0:
  12.8 47.7 all-gather.5
  185.4 63.5 all-gather.7
where the time goes:
time: 263 us
  blocking collectives  148 us (56%)
  waiting for transfers between devices  75.5 us (29%)
  between operations  15 us (6%)
  matrix products  11.3 us (4%)
  local copies, waits for them, and re-layouts  11.2 us (4%)
    psum x1, blocking collectives, per_device(): square_sum = lax.psum(jnp.sum(attn_f * attn_f, axis=(1, 2)), 'head')  61.6 us
    all_gather x1, waiting for transfers between devices, per_device(): lax.all_gather(start_state[None], 'ctx', axis=0, tiled=True)  60.8 us
    psum x1, blocking collectives, per_device(): inner = lax.psum(jnp.sum(scaled_grad * attn_f, axis=(1, 2)), 'head')  56.2 us
    unnamed x1, blocking collectives  29.7 us
    all_gather x1, waiting for transfers between devices, per_device(): lax.all_gather(end_state[None], 'ctx', axis=0, tiled=True)  14.7 us
    unnamed x22, local copies, waits for them, and re-layouts  8.56 us
    dot_general x2, matrix products, weigh_gathered(): jnp.einsum('nh,nhde->hde', factors, gathered, precision=lax.Precision.HIG...  7.53 us
  transfers between devices with their start and end apart: 2, of which 2 were waited for; matrix products, arithmetic and copies ran while one was open for 2% of the time, Pallas kernels for 0%

commit v1 on v0

--- a/solution.py
+++ b/solution.py
@@ -60,8 +60,14 @@
     )
     total_log = jnp.sum(block_total, axis=0)
     position = lax.axis_index("ctx")
+
+    def map_skins(group_axis, arr):
+        res = jnp.stack([arr for _ in range(lax.axis_size(group_axis))], 0)
+        raw_out = lax.all_to_all(res, axis_name=group_axis, split_axis=0, concat_axis=0)
+        return jnp.concatenate(raw_out, 0)
+
     gathered, log_rates = (
-        lax.all_gather(end_state[None], "ctx", axis=0, tiled=True),
+        map_skins("ctx", arr=end_state[None]),
         lax.all_gather(total_log[None], "ctx", axis=0, tiled=True),
     )
     incoming = weigh_gathered(gathered, log_rates, position, True)

time: 263 us -> 305 us (1.16)
  blocking collectives: 148 us -> 185 us
  waiting for transfers between devices: 75.5 us -> 62.2 us
  starting transfers between devices: 0.08 us -> 10.5 us
  local copies, waits for them, and re-layouts: 11.2 us -> 16.6 us
    unnamed x1, blocking collectives: 29.7 us -> 63.9 us
    all_gather x1 -> x0, waiting for transfers between devices: 14.7 us -> none  [per_device(): lax.all_gather(end_state[None], 'ctx', axis=0, tiled=True)]
    all_to_all x0 -> x1, starting transfers between devices: none -> 10.5 us  [map_skins(): lax.all_to_all(res, axis_name=group_axis, split_axis=0, concat_axis=0)]
    psum x1, blocking collectives: 61.6 us -> 65.3 us  [per_device(): square_sum = lax.psum(jnp.sum(attn_f * attn_f, axis=(1, 2)), 'head')]
    unnamed x22 -> x44, local copies, waits for them, and re-layouts: 8.56 us -> 9.16 us
  transfers between devices with their start and end apart: 2 -> 2, of which waited for: 2 -> 1; matrix products, arithmetic and copies ran while one was open for 2% -> 3% of each run, Pallas kernels for 0% -> 0%
where the time goes in v1:
time: 305 us
  blocking collectives  185 us (61%)
  waiting for transfers between devices  62.2 us (20%)
  local copies, waits for them, and re-layouts  16.6 us (5%)
  between operations  15.1 us (5%)
  matrix products  11.2 us (4%)
  starting transfers between devices  10.5 us (3%)
  other arithmetic  3.37 us (1%)
    psum x1, blocking collectives, per_device(): square_sum = lax.psum(jnp.sum(attn_f * attn_f, axis=(1, 2)), 'head')  65.3 us
    unnamed x1, blocking collectives  63.9 us
    all_gather x1, waiting for transfers between devices, per_device(): lax.all_gather(start_state[None], 'ctx', axis=0, tiled=True)  62.2 us
    psum x1, blocking collectives, per_device(): inner = lax.psum(jnp.sum(scaled_grad * attn_f, axis=(1, 2)), 'head')  56.1 us
    all_to_all x1, starting transfers between devices, map_skins(): lax.all_to_all(res, axis_name=group_axis, split_axis=0, concat_axis=0)  10.5 us
    unnamed x44, local copies, waits for them, and re-layouts  9.16 us
    dot_general x2, matrix products, weigh_gathered(): jnp.einsum('nh,nhde->hde', factors, gathered, precision=lax.Precision.HIG...  6.7 us
  transfers between devices with their start and end apart: 2, of which 1 were waited for; matrix products, arithmetic and copies ran while one was open for 3% of the time, Pallas kernels for 0%

profile of v1, /device:TPU:1, one launch (start us, length us, event | category | flops | bytes accessed | tf_op | source)
XLA Modules:
  0.0 304.6 jit_solution(9493013690401350437)
XLA Ops:
  7.2 0.8 copy.129
  8.5 1.0 copy.85
  9.5 1.0 copy.79
  10.5 1.4 while.30
  11.9 1.6 stack.3
  13.5 10.5 %all-to-all-start = ((f32[16,1,2,128,128]{4,3,2,1,0:T(8,128)}), f32[16,1,2,128,128]{4,3,2,1,0:T(8,128)S(1)}, u32[]{:S(2)}, u32[]{:S(2)}) async-start(f32[16,1,2,128,128]{4,3,2,1,0:T(8,128)} %stack.3), calls=%async_computation | async-start | bytes 4194304 | tf_op jit(solution)/shard_map/all_to_all | solution.py:66
  24.0 1.3 dynamic-slice
  26.2 63.9 %all-reduce = f32[32]{0:T(128)S(1)} all-reduce(f32[32]{0:T(128)S(1)} %dynamic-update-slice), channel_id=2, replica_groups=mesh['ctx'=16,'head'=32] {'ctx'}, use_global_device_ids=true, to_apply=%add | all-reduce | flops 32 | bytes 256
  91.2 1.3 subtract_exponential_fusion.1
  93.1 0.7 subtract_exponential_fusion
  93.9 1.0 copy.78
  95.7 2.9 fusion.24
  98.6 1.0 fusion.27
  99.9 65.3 %psum.14 = f32[384]{0:T(512)S(1)} all-reduce(f32[384]{0:T(512)S(1)} %bitcast.171), channel_id=1, replica_groups=mesh['ctx'=16,'head'=32] {'head'}, use_global_device_ids=true, to_apply=%region_7.8 | all-reduce | flops 384 | bytes 3072 | tf_op jit(solution)/shard_map/psum | solution.py:88
  165.4 56.1 %psum.15 = f32[384]{0:T(512)S(1)} all-reduce(f32[384]{0:T(512)S(1)} %fusion.43), channel_id=1, replica_groups=mesh['ctx'=16,'head'=32] {'head'}, use_global_device_ids=true, to_apply=%region_9.10 | all-reduce | flops 384 | bytes 3072 | tf_op jit(solution)/shard_map/psum | solution.py:92
  221.9 3.3 %while.31 = (s32[]{:T(128)}, f32[2,128,128]{2,1,0:T(8,128)S(1)}, f32[3,2,128,128]{3,2,1,0:T(8,128)S(1)}, f32[3,2]{1,0:T(4,128)}, bf16[3,128,2,128]{3,1,0,2:T(8,1...) while((s32[]{:T(128)}, f32[2,128,128]{2,1,0:T(8,128)S(1)}, ...), condition=%wide.region_11.12_spmd.clone, body=%wide.region_10.11_spmd.clone.sunk | while | flops 8617988 | bytes 921248 | solution.py:124
  222.1 0.7 fusion.84
  224.3 0.7 fusion.84
  227.0 0.9 copy.118
  227.9 0.9 copy.117
  228.7 62.2 %all-gather.4.cloned.1.call-done = f32[32,128,128]{2,1,0:T(8,128)} async-done(((f32[2,128,128]{2,1,0:T(8,128)}), f32[32,128,128]{2,1,0:T(8,128)}) %all-gather.4.cloned.1.call-update) | async-done | bytes 2097168 | tf_op jit(solution)/shard_map/all_gather | solution.py:128
  291.0 3.8 %fusion.22 = f32[2,1,128,128]{3,1,2,0:T(1,128)S(1)} fusion(f32[16,2,1,1]{0,2,3,1:T(1,128)S(1)} %copy.125, f32[16,2,128,128]{3,2,1,0:T(8,128)} %bitcast.160), kind=kOutput, calls=%fused_computation.32 | convolution fusion | flops 6291456 | bytes 2228352 | tf_op jit(solution)/shard_map/nh,nhde->hde/dot_general | solution.py:22
  295.7 0.9 copy.120
  296.9 0.9 copy.119
  (113 shorter events, 10.1 us)
Async XLA Ops:
  8.2 17.7 %copy-start.15 = (f32[2]{0:T(128)}, f32[2]{0:T(128)S(1)}, u32[]{:S(2)}) copy-start(f32[2]{0:T(128)S(1)} %get-tuple-element.320) | copy-start | bytes 28
  8.4 2.1 copy-start.9
  11.9 81.2 %copy-start.5 = (f32[3,2]{1,0:T(4,128)}, f32[3,2]{1,0:T(4,128)S(1)}, u32[]{:S(2)}) copy-start(f32[3,2]{1,0:T(4,128)S(1)} %get-tuple-element.489) | copy-start | bytes 76
  13.5 77.5 %copy-start.10 = (f32[3,1,2]{0,2,1:T(2,128)S(1)}, f32[3,1,2]{0,2,1:T(2,128)}, u32[]{:S(2)}) copy-start(f32[3,1,2]{0,2,1:T(2,128)} %copy-done.9) | copy-start | bytes 76
  13.5 81.9 %all-to-all-start = ((f32[16,1,2,128,128]{4,3,2,1,0:T(8,128)}), f32[16,1,2,128,128]{4,3,2,1,0:T(8,128)S(1)}, u32[]{:S(2)}, u32[]{:S(2)}) async-start(f32[16,1,2,128,128]{4,3,2,1,0:T(8,128)} %stack.3), calls=%async_computation | async-start | bytes 4194304 | tf_op jit(solution)/shard_map/all_to_all | solution.py:66
  24.0 267.0 %all-gather.4.cloned.1.call-start = ((), (), s32[]{:S(2)}) async-start(), calls=%async_computation.1 | async-start | bytes 2228224 | tf_op jit(solution)/shard_map/all_gather | solution.py:128
  95.0 0.6 copy-start.13
  95.0 0.6 copy-start.7
  95.3 4.6 %copy-start.3 = (bf16[3,2,128,128]{3,2,1,0:T(8,128)(2,1)}, bf16[3,2,128,128]{3,2,1,0:T(8,128)(2,1)S(1)}, u32[]{:S(2)}) copy-start(bf16[3,2,128,128]{3,2,1,0:T(8,128)(2,1)S(1)} %fusion.34) | copy-start | bytes 589828
  98.6 66.6 %copy-start.2 = (bf16[384,2,128]{2,1,0:T(2,128)(2,1)S(1)}, bf16[384,2,128]{2,1,0:T(2,128)(2,1)}, u32[]{:S(2)}) copy-start(bf16[384,2,128]{2,1,0:T(2,128)(2,1)} %param.15) | copy-start | bytes 589828
  98.6 66.6 %copy-start.11 = (f32[2,128]{1,0:T(2,128)S(1)}, f32[2,128]{1,0:T(2,128)}, u32[]{:S(2)}) copy-start(f32[2,128]{1,0:T(2,128)} %param.14) | copy-start | bytes 3076
  221.8 4.1 %copy-start.12 = (f32[3,2]{0,1:T(2,128)S(1)}, f32[3,2]{0,1:T(2,128)}, u32[]{:S(2)}) copy-start(f32[3,2]{0,1:T(2,128)} %get-tuple-element.326) | copy-start | bytes 76
  221.8 4.2 %copy-start.1 = (f32[3,128,2]{2,1,0:T(8,128)S(1)}, f32[3,128,2]{2,1,0:T(8,128)}, u32[]{:S(2)}) copy-start(f32[3,128,2]{2,1,0:T(8,128)} %get-tuple-element.318) | copy-start | bytes 9220
  221.9 4.2 %copy-start.8 = (pred[128,128]{1,0:T(8,128)(4,1)S(1)}, pred[128,128]{1,0:T(8,128)(4,1)}, u32[]{:S(2)}) copy-start(pred[128,128]{1,0:T(8,128)(4,1)} %copy-done.7) | copy-start | bytes 49156
  221.9 4.2 %copy-start.14 = (f32[3,2,128]{2,1,0:T(2,128)S(1)}, f32[3,2,128]{2,1,0:T(2,128)}, u32[]{:S(2)}) copy-start(f32[3,2,128]{2,1,0:T(2,128)} %copy-done.13) | copy-start | bytes 9220
  221.9 4.5 %copy-start.6 = (f32[3,2]{1,0:T(4,128)S(1)}, f32[3,2]{1,0:T(4,128)}, u32[]{:S(2)}) copy-start(f32[3,2]{1,0:T(4,128)} %copy.92) | copy-start | bytes 76
  225.2 0.7 copy-start
  291.0 4.4 %copy-start.4 = (bf16[3,2,128,128]{3,2,1,0:T(8,128)(2,1)S(1)}, bf16[3,2,128,128]{3,2,1,0:T(8,128)(2,1)}, u32[]{:S(2)}) copy-start(bf16[3,2,128,128]{3,2,1,0:T(8,128)(2,1)} %copy-done.3) | copy-start | bytes 589828
Sparse Core Ops, SparseCore 0:
  226.0 64.9 all-gather.3
